TPU v7x, 256 devices: a whole 4x4x8 slice. The times are simulated.
256 devices in a mesh: blk: 32 (over z, y), view: 8 (over x, core).
Axes of the slice: x: 4, y: 4, z: 8, core: 2. Of those that a mesh axis runs over, the one named last changes fastest.
Arguments:
- estimate: float32 [512, 128, 256], P('blk'), may hold values from 0.3 to 3
- views: float32 [8, 512, 128, 256], P('view', 'blk'), may hold values from 0.3 to 3
- axial_taps: float32 [8, 33], P('view'), may hold values from 0.1 to 1
- lateral_taps: float32 [8, 2, 17], P('view'), may hold values from 0.05 to 1
- cover: int32 [8, 2], P('view'), may hold values from 0 to 512, as said below
Outputs:
- refined: float32 [512, 128, 256], P('blk')
Inputs may be any that keep to these rules, and one draw needn't show every extreme that they name: cover[v, 0] < cover[v, 1]; every first plane is at most 128 and every end at least 384; some view starts at plane 0 and some view ends at 512.
All inputs are finite; a program needn't handle non-finite values.
Results may differ from a plain program's by a relative error of at most 0.00015.
Values sent between devices are 32-bit elements; how exact they have to be, the bound alone decides.
No kernel may reach another device: no remote copies, remote signals or barrier semaphores. Data moves between devices by JAX's collectives and lax.ppermute only.
A program may use at most 64 MiB of HBM per device.

v0:
```python
import jax
import jax.numpy as jnp
from jax import lax
from jax.sharding import PartitionSpec as P

RAD = 8
RZ = 16
ITERS = 2


def padded(block, sides, width):
    for axis, dim in sides:
        count = lax.axis_size(axis)
        forward = [(i, i + 1) for i in range(count - 1)]
        backward = [(target, source) for source, target in forward]
        low = lax.ppermute(
            lax.slice_in_dim(block, block.shape[dim] - width, None, axis=dim), axis, forward
        )
        high = lax.ppermute(lax.slice_in_dim(block, 0, width, axis=dim), axis, backward)
        block = jnp.concatenate([low, block, high], axis=dim)
    return block


def banded(taps, count, reach):
    taps = taps / jnp.sum(taps)
    rows = jnp.arange(count)[:, None]
    cols = jnp.arange(count)[None, :]
    offset = cols - rows
    where_in = jnp.abs(offset) <= reach
    index = jnp.clip(offset + reach, 0, 2 * reach)
    return jnp.where(where_in, jnp.take(taps, index), jnp.float32(0.0))


def local_axial(taps, planes_dev, reach, flipped):
    taps = taps / jnp.sum(taps)
    rows = jnp.arange(planes_dev)[:, None]
    cols = jnp.arange(planes_dev + 2 * reach)[None, :]
    if flipped:
        offset = rows + reach - cols
    else:
        offset = cols - reach - rows
    where_in = jnp.abs(offset) <= reach
    index = jnp.clip(offset + reach, 0, 2 * reach)
    return jnp.where(where_in, jnp.take(taps, index), jnp.float32(0.0))


def local(estimate, views, axial_taps, lateral_taps, cover):
    hi = lax.Precision.HIGHEST
    planes_dev, rows_all, cols_all = estimate.shape
    ky = banded(lateral_taps[0, 0], rows_all, RAD)
    kx = banded(lateral_taps[0, 1], cols_all, RAD)
    planes = lax.axis_index("blk") * planes_dev + jnp.arange(planes_dev)
    inside = (planes >= cover[0, 0]) & (planes < cover[0, 1])
    recorded = views[0]
    kz_ahead = local_axial(axial_taps[0], planes_dev, RZ, False)
    kz_behind = local_axial(axial_taps[0], planes_dev, RZ, True)
    for step in range(ITERS):
        widened = padded(estimate, (("blk", 0),), RZ)
        blurred = jnp.einsum("wc,cyx->wyx", kz_ahead, widened, precision=hi)
        blurred = jnp.einsum("zyx,wx->zyw", blurred, kx, precision=hi)
        blurred = jnp.einsum("zyx,wy->zwx", blurred, ky, precision=hi)
        ratio = recorded / blurred
        back = jnp.einsum("zyx,xw->zyw", ratio, kx, precision=hi)
        back = jnp.einsum("zyx,yw->zwx", back, ky, precision=hi)
        spread = padded(back, (("blk", 0),), RZ)
        returned = jnp.einsum("wc,cyx->wyx", kz_behind, spread, precision=hi)
        log_terms = jnp.where(inside[:, None, None], jnp.log(returned), jnp.float32(0.0))
        total = lax.psum(log_terms, "view")
        estimate = estimate * jnp.exp(total)
    return estimate


def solution(mesh):
    in_specs = (
        P("blk", None, None),
        P("view", "blk", None, None),
        P("view", None),
        P("view", None, None),
        P("view", None),
    )
    out_specs = P("blk", None, None)
    return jax.shard_map(local, mesh=mesh, in_specs=in_specs, out_specs=out_specs, check_vma=False)
```

profile of v0, /device:TPU:8, one launch (start us, length us, event | category | flops | bytes accessed | tf_op | source)
XLA Modules:
  0.0 520.1 jit_solution(3957215918461065242)
XLA Ops:
  6.5 0.0 all-reduce.3.cloned.1.call-start
  6.5 4.1 collective-permute-start.1
  10.6 1.9 collective-permute-start
  12.6 0.1 reshape.362
  12.7 1.3 reduce_sum.27
  13.9 1.3 divide_bitcast_fusion
  15.2 0.0 copy-start.1
  15.2 4.8 gather_fusion.1
  20.0 0.1 reshape.365
  20.1 0.0 copy-done.1
  20.1 0.6 slice_reduce_fusion.1
  20.7 1.2 slice_divide_fusion.1
  21.9 0.7 fusion.312
  22.6 0.7 fusion.313
  23.4 32.7 %collective-permute-done.1 = f32[16,128,256]{2,1,0:T(8,128)} collective-permute-done((f32[16,128,256]{2,1,0:T(8,128)}, f32[16,128,256]{2,1,0:T(8,128)}, u32[]{:S(2)}, u32[]{:S(2)}) %collective-permute-start.1) | collective-permute-done | bytes 2097184 | tf_op jit(solution)/shard_map/ppermute | solution.py:19
  56.1 1.9 collective-permute-done
  58.0 0.0 copy-done
  58.0 3.0 pad_maximum_fusion
  61.1 6.6 %fusion.6 = f32[16,128,256]{2,0,1:T(8,128)S(1)} fusion(f32[48,128,256]{2,1,0:T(8,128)S(1)} %pad_maximum_fusion, f32[16,48]{1,0:T(8,128)S(1)} %reshape.365, s32[48]{0:T(128)S(1)} %iota_add_fusion), kind=kOutput, calls=%fused_computation.11 | convolution fusion | flops 301999872 | bytes 8391872 | tf_op jit(solution)/shard_map/wc,cyx->wyx/dot_general | solution.py:59
  67.6 13.7 %fusion.18 = f32[16,128,256]{2,1,0:T(8,128)S(1)} fusion(f32[16,128,256]{2,0,1:T(8,128)S(1)} %fusion.6, f32[]{:T(128)} %bitcast.55, f32[]{:T(128)} %bitcast.56, f32[]{:T(128)} %bitcast.57, f32[]{:T(128)} %bitcast.58, f32[]{:T(128)} %bitcast.59, f32[]{:T(128)} %bitcast.61, f32[]{:T(128)} %bitcast.60, f32[]{:T(128)} %bitcast.36, f32[]{:T(128)} %bitcast.38, ...), kind=kOutput, calls=%fused_computation.25 | convolution fusion | flops 1613955072 | bytes 4194372 | tf_op jit(solution)/shard_map/zyx,wx->zyw/dot_general | solution.py:60
  81.3 0.0 copy-start.3
  81.4 13.1 %fusion.76 = f32[128,16,256]{2,0,1:T(8,128)S(1)} fusion(f32[16,128,256]{2,1,0:T(8,128)S(1)} %fusion.18, f32[]{:T(128)} %bitcast.24, f32[]{:T(128)} %bitcast.25, f32[]{:T(128)} %bitcast.26, f32[]{:T(128)} %bitcast.27, f32[]{:T(128)} %bitcast.28, f32[]{:T(128)} %bitcast.30, f32[]{:T(128)} %bitcast.29, f32[]{:T(128)} %bitcast.5, f32[]{:T(128)} %bitcast.7, ...), kind=kOutput, calls=%fused_computation.88 | convolution fusion | flops 806141952 | bytes 4194372 | tf_op jit(solution)/shard_map/zyx,wy->zwx/dot_general | solution.py:61
  94.4 0.0 copy-done.3
  94.4 12.7 %fusion.13 = f32[16,128,256]{2,1,0:T(8,128)S(1)} fusion(f32[128,16,256]{2,0,1:T(8,128)S(1)} %fusion.76, f32[1,16,128,256]{3,2,1,0:T(8,128)S(1)} %copy-done.3, f32[]{:T(128)} %bitcast.55, f32[]{:T(128)} %bitcast.56, f32[]{:T(128)} %bitcast.57, f32[]{:T(128)} %bitcast.58, f32[]{:T(128)} %bitcast.59, f32[]{:T(128)} %bitcast.61, f32[]{:T(128)} %bitcast.60, ...), kind=kOutput, calls=%fused_computation.20 | convolution fusion | flops 1614479360 | bytes 6291524 | tf_op jit(solution)/shard_map/zyx,xw->zyw/dot_general | solution.py:63
  107.1 12.7 %convolution_bitcast_fusion.1 = f32[16,128,256]{2,1,0:T(8,128)S(1)} fusion(f32[16,128,256]{2,1,0:T(8,128)S(1)} %fusion.13, f32[]{:T(128)} %bitcast.24, f32[]{:T(128)} %bitcast.25, f32[]{:T(128)} %bitcast.26, f32[]{:T(128)} %bitcast.27, f32[]{:T(128)} %bitcast.28, f32[]{:T(128)} %bitcast.30, f32[]{:T(128)} %bitcast.29, f32[]{:T(128)} %bitcast.5, ...), kind=kOutput, calls=%fused_computation.32 | convolution fusion | flops 806141952 | bytes 4194372 | tf_op jit(solution)/shard_map/zyx,yw->zwx/dot_general | solution.py:64
  119.9 1.9 collective-permute-start.3
  121.8 3.9 collective-permute-start.2
  125.7 0.1 compare_select_fusion.5
  125.8 0.1 reshape.358
  125.9 0.0 copy-start.2
  125.9 4.8 gather_fusion
  130.7 0.1 reshape.361
  130.8 0.0 copy-done.2
  130.8 0.6 fusion.311
  131.3 1.2 compare_and_fusion
  132.5 35.3 %collective-permute-done.3 = f32[16,128,256]{2,1,0:T(8,128)} collective-permute-done((f32[16,128,256]{2,1,0:T(8,128)S(1)}, f32[16,128,256]{2,1,0:T(8,128)}, u32[]{:S(2)}, u32[]{:S(2)}) %collective-permute-start.3) | collective-permute-done | bytes 2097184 | tf_op jit(solution)/shard_map/ppermute | solution.py:19
  167.9 1.2 collective-permute-done.2
  169.0 3.0 pad_maximum_fusion.1
  172.0 7.8 %log_select_fusion.1 = f32[16,128,256]{2,0,1:T(8,128)} fusion(f32[48,128,256]{2,1,0:T(8,128)S(1)} %pad_maximum_fusion.1, pred[16]{0:T(512)(128)(4,1)S(1)} %compare_and_fusion, f32[16,48]{1,0:T(8,128)S(1)} %reshape.361, s32[16]{0:T(128)S(1)} %iota_add_fusion.1), kind=kOutput, calls=%fused_computation.30 | convolution fusion | flops 302524160 | bytes 8391760 | tf_op jit(solution)/shard_map/wc,cyx->wyx/dot_general | solution.py:66
  179.9 0.0 all-reduce.3.cloned.1.call-update
  179.9 0.0 all-reduce.5.cloned.1.call-start
  179.9 80.9 %all-reduce.3.cloned.1.call-done = f32[16,128,256]{2,0,1:T(8,128)} async-done(((f32[16,128,256]{2,0,1:T(8,128)}), f32[16,128,256]{2,0,1:T(8,128)}) %all-reduce.3.cloned.1.call-update) | async-done | bytes 2097168 | tf_op jit(solution)/shard_map/psum | solution.py:68
  260.8 3.6 copy_multiply_fusion
  264.4 2.4 collective-permute-start.5
  266.9 3.8 collective-permute-start.4
  270.7 41.1 %collective-permute-done.5 = f32[16,128,256]{2,0,1:T(8,128)S(1)} collective-permute-done((f32[16,128,256]{2,0,1:T(8,128)S(1)}, f32[16,128,256]{2,0,1:T(8,128)S(1)}, u32[]{:S(2)}, u32[]{:S(2)}) %collective-permute-start.5) | collective-permute-done | bytes 2097184 | tf_op jit(solution)/shard_map/ppermute | solution.py:19
  311.8 2.2 collective-permute-done.4
  313.9 3.1 fusion
  317.1 13.8 %fusion.16 = f32[16,128,256]{2,1,0:T(8,128)S(1)} fusion(f32[16,128,256]{2,0,1:T(8,128)S(1)} %fusion, f32[]{:T(128)} %bitcast.55, f32[]{:T(128)} %bitcast.56, f32[]{:T(128)} %bitcast.57, f32[]{:T(128)} %bitcast.58, f32[]{:T(128)} %bitcast.59, f32[]{:T(128)} %bitcast.61, f32[]{:T(128)} %bitcast.60, f32[]{:T(128)} %bitcast.36, f32[]{:T(128)} %bitcast.38, ...), kind=kOutput, calls=%fused_computation.23 | convolution fusion | flops 1613955072 | bytes 4194372 | tf_op jit(solution)/shard_map/zyx,wx->zyw/dot_general | solution.py:60
  330.8 0.0 copy-start.4
  330.9 12.9 %fusion.73 = f32[128,16,256]{2,0,1:T(8,128)S(1)} fusion(f32[16,128,256]{2,1,0:T(8,128)S(1)} %fusion.16, f32[]{:T(128)} %bitcast.24, f32[]{:T(128)} %bitcast.25, f32[]{:T(128)} %bitcast.26, f32[]{:T(128)} %bitcast.27, f32[]{:T(128)} %bitcast.28, f32[]{:T(128)} %bitcast.30, f32[]{:T(128)} %bitcast.29, f32[]{:T(128)} %bitcast.5, f32[]{:T(128)} %bitcast.7, ...), kind=kOutput, calls=%fused_computation.85 | convolution fusion | flops 806141952 | bytes 4194372 | tf_op jit(solution)/shard_map/zyx,wy->zwx/dot_general | solution.py:61
  343.7 0.0 copy-done.4
  343.7 12.8 %fusion.12 = f32[16,128,256]{2,1,0:T(8,128)S(1)} fusion(f32[128,16,256]{2,0,1:T(8,128)S(1)} %fusion.73, f32[1,16,128,256]{3,2,1,0:T(8,128)S(1)} %copy-done.4, f32[]{:T(128)} %bitcast.55, f32[]{:T(128)} %bitcast.56, f32[]{:T(128)} %bitcast.57, f32[]{:T(128)} %bitcast.58, f32[]{:T(128)} %bitcast.59, f32[]{:T(128)} %bitcast.61, f32[]{:T(128)} %bitcast.60, ...), kind=kOutput, calls=%fused_computation.18 | convolution fusion | flops 1614479360 | bytes 6291524 | tf_op jit(solution)/shard_map/zyx,xw->zyw/dot_general | solution.py:63
  356.5 12.9 %convolution_bitcast_fusion = f32[16,128,256]{2,1,0:T(8,128)S(1)} fusion(f32[16,128,256]{2,1,0:T(8,128)S(1)} %fusion.12, f32[]{:T(128)} %bitcast.24, f32[]{:T(128)} %bitcast.25, f32[]{:T(128)} %bitcast.26, f32[]{:T(128)} %bitcast.27, f32[]{:T(128)} %bitcast.28, f32[]{:T(128)} %bitcast.30, f32[]{:T(128)} %bitcast.29, f32[]{:T(128)} %bitcast.5, f32[]{:T(128)} %bitcast.7, ...), kind=kOutput, calls=%fused_computation.31 | convolution fusion | flops 806141952 | bytes 4194372 | tf_op jit(solution)/shard_map/zyx,yw->zwx/dot_general | solution.py:64
  369.5 1.9 collective-permute-start.7
  371.4 3.9 collective-permute-start.6
  375.3 40.3 %collective-permute-done.7 = f32[16,128,256]{2,1,0:T(8,128)S(1)} collective-permute-done((f32[16,128,256]{2,1,0:T(8,128)S(1)}, f32[16,128,256]{2,1,0:T(8,128)S(1)}, u32[]{:S(2)}, u32[]{:S(2)}) %collective-permute-start.7) | collective-permute-done | bytes 2097184 | tf_op jit(solution)/shard_map/ppermute | solution.py:19
  415.6 1.9 collective-permute-done.6
  417.5 0.7 pad_maximum_fusion.2
  418.2 7.8 %log_select_fusion = f32[16,128,256]{2,0,1:T(8,128)} fusion(f32[48,128,256]{2,1,0:T(8,128)S(1)} %pad_maximum_fusion.2, pred[16]{0:T(512)(128)(4,1)S(1)} %compare_and_fusion, f32[16,48]{1,0:T(8,128)S(1)} %reshape.361, s32[16]{0:T(128)S(1)} %iota_add_fusion.1), kind=kOutput, calls=%fused_computation.29 | convolution fusion | flops 302524160 | bytes 8391760 | tf_op jit(solution)/shard_map/wc,cyx->wyx/dot_general | solution.py:66
  426.0 0.0 all-reduce.5.cloned.1.call-update
  426.1 82.3 %all-reduce.5.cloned.1.call-done = f32[16,128,256]{2,0,1:T(8,128)} async-done(((f32[16,128,256]{2,0,1:T(8,128)}), f32[16,128,256]{2,0,1:T(8,128)}) %all-reduce.5.cloned.1.call-update) | async-done | bytes 2097168 | tf_op jit(solution)/shard_map/psum | solution.py:68
  508.4 2.1 exponential_multiply_fusion
  510.5 2.5 copy.13
  (6 shorter events, 0.0 us)
Async XLA Ops:
  6.5 254.3 %all-reduce.3.cloned.1.call-start = ((), (), s32[]{:S(2)}) async-start(), calls=%async_computation | async-start | bytes 4194304 | tf_op jit(solution)/shard_map/psum | solution.py:68
  6.5 49.6 %collective-permute-start.1 = (f32[16,128,256]{2,1,0:T(8,128)}, f32[16,128,256]{2,1,0:T(8,128)}, u32[]{:S(2)}, u32[]{:S(2)}) collective-permute-start(f32[16,128,256]{2,1,0:T(8,128)} %param.7), channel_id=1, source_target_pairs={{8,0},{16,8},{24,16},{32,24},{40,32},{48,40},{56,48},{64,56},{72,6... | collective-permute-start | bytes 6291464 | tf_op jit(solution)/shard_map/ppermute | solution.py:19
  10.6 47.4 %collective-permute-start = (f32[16,128,256]{2,1,0:T(8,128)}, f32[16,128,256]{2,1,0:T(8,128)}, u32[]{:S(2)}, u32[]{:S(2)}) collective-permute-start(f32[16,128,256]{2,1,0:T(8,128)} %param.7), channel_id=1, source_target_pairs={{0,8},{8,16},{16,24},{24,32},{32,40},{40,48},{48,56},{56,64},{64,7... | collective-permute-start | bytes 6291464 | tf_op jit(solution)/shard_map/ppermute | solution.py:16
  15.2 4.9 copy-start.1
  15.2 42.8 %copy-start = (f32[16,128,256]{2,1,0:T(8,128)S(1)}, f32[16,128,256]{2,1,0:T(8,128)}, u32[]{:S(2)}) copy-start(f32[16,128,256]{2,1,0:T(8,128)} %param.7) | copy-start | bytes 6291460
  81.3 13.1 %copy-start.3 = (f32[1,16,128,256]{3,2,1,0:T(8,128)S(1)}, f32[1,16,128,256]{3,2,1,0:T(8,128)}, u32[]{:S(2)}) copy-start(f32[1,16,128,256]{3,2,1,0:T(8,128)} %param.8) | copy-start | bytes 6291460
  119.9 48.0 %collective-permute-start.3 = (f32[16,128,256]{2,1,0:T(8,128)S(1)}, f32[16,128,256]{2,1,0:T(8,128)}, u32[]{:S(2)}, u32[]{:S(2)}) collective-permute-start(f32[16,128,256]{2,1,0:T(8,128)S(1)} %convolution_bitcast_fusion.1), channel_id=1, source_target_pairs={{8,0},{16,8},{24,16},{32,24},{40,32},{48,40},{56,48},{64,56},{72,6... | collective-permute-start | bytes 6291464 | tf_op jit(solution)/shard_map/ppermute | solution.py:19
  121.8 47.2 %collective-permute-start.2 = (f32[16,128,256]{2,1,0:T(8,128)S(1)}, f32[16,128,256]{2,1,0:T(8,128)}, u32[]{:S(2)}, u32[]{:S(2)}) collective-permute-start(f32[16,128,256]{2,1,0:T(8,128)S(1)} %convolution_bitcast_fusion.1), channel_id=1, source_target_pairs={{0,8},{8,16},{16,24},{24,32},{32,40},{40,48},{48,56},{56,64},{64,7... | collective-permute-start | bytes 6291464 | tf_op jit(solution)/shard_map/ppermute | solution.py:16
  125.9 4.9 copy-start.2
  179.9 328.5 %all-reduce.5.cloned.1.call-start = ((), (), s32[]{:S(2)}) async-start(), calls=%async_computation.1 | async-start | bytes 4194304 | tf_op jit(solution)/shard_map/psum | solution.py:68
  264.4 47.3 %collective-permute-start.5 = (f32[16,128,256]{2,0,1:T(8,128)S(1)}, f32[16,128,256]{2,0,1:T(8,128)S(1)}, u32[]{:S(2)}, u32[]{:S(2)}) collective-permute-start(f32[16,128,256]{2,0,1:T(8,128)S(1)} %copy_multiply_fusion), channel_id=1, source_target_pairs={{8,0},{16,8},{24,16},{32,24},{40,32},{48,40},{56,48},{64,56},{72,6... | collective-permute-start | bytes 6291464 | tf_op jit(solution)/shard_map/ppermute | solution.py:19
  266.9 47.1 %collective-permute-start.4 = (f32[16,128,256]{2,0,1:T(8,128)S(1)}, f32[16,128,256]{2,0,1:T(8,128)S(1)}, u32[]{:S(2)}, u32[]{:S(2)}) collective-permute-start(f32[16,128,256]{2,0,1:T(8,128)S(1)} %copy_multiply_fusion), channel_id=1, source_target_pairs={{0,8},{8,16},{16,24},{24,32},{32,40},{40,48},{48,56},{56,64},{64,7... | collective-permute-start | bytes 6291464 | tf_op jit(solution)/shard_map/ppermute | solution.py:16
  330.8 12.9 %copy-start.4 = (f32[1,16,128,256]{3,2,1,0:T(8,128)S(1)}, f32[1,16,128,256]{3,2,1,0:T(8,128)}, u32[]{:S(2)}) copy-start(f32[1,16,128,256]{3,2,1,0:T(8,128)} %param.8) | copy-start | bytes 6291460
  369.5 46.1 %collective-permute-start.7 = (f32[16,128,256]{2,1,0:T(8,128)S(1)}, f32[16,128,256]{2,1,0:T(8,128)S(1)}, u32[]{:S(2)}, u32[]{:S(2)}) collective-permute-start(f32[16,128,256]{2,1,0:T(8,128)S(1)} %convolution_bitcast_fusion), channel_id=1, source_target_pairs={{8,0},{16,8},{24,16},{32,24},{40,32},{48,40},{56,48},{64,56},{72,6... | collective-permute-start | bytes 6291464 | tf_op jit(solution)/shard_map/ppermute | solution.py:19
  371.4 46.1 %collective-permute-start.6 = (f32[16,128,256]{2,1,0:T(8,128)S(1)}, f32[16,128,256]{2,1,0:T(8,128)S(1)}, u32[]{:S(2)}, u32[]{:S(2)}) collective-permute-start(f32[16,128,256]{2,1,0:T(8,128)S(1)} %convolution_bitcast_fusion), channel_id=1, source_target_pairs={{0,8},{8,16},{16,24},{24,32},{32,40},{40,48},{48,56},{56,64},{64,7... | collective-permute-start | bytes 6291464 | tf_op jit(solution)/shard_map/ppermute | solution.py:16
Sparse Core Ops, SparseCore 0:
  180.0 80.7 all-reduce.2
  426.2 82.1 all-reduce.4
where the time goes:
time: 531 us; the launch traced here: 520 us
  waiting for transfers between devices  320 us (60%)
  matrix products  130 us (24%)
  starting transfers between devices  24 us (5%)
  other arithmetic  18.1 us (3%)
  local copies, waits for them, and re-layouts  14.4 us (3%)
  between operations  13.9 us (3%)
    psum x2, waiting for transfers between devices, local(): total = lax.psum(log_terms, 'view')  163 us
    ppermute x4, waiting for transfers between devices, padded(): lax.ppermute(lax.slice_in_dim(block, 0, width, axis=dim), axis, backward)  149 us
    dot_general x2, matrix products, local(): blurred = jnp.einsum('zyx,wx->zyw', blurred, kx, precision=hi)  27.5 us
    dot_general x2, matrix products, local(): blurred = jnp.einsum('zyx,wy->zwx', blurred, ky, precision=hi)  25.9 us
    dot_general x2, matrix products, local(): back = jnp.einsum('zyx,yw->zwx', back, ky, precision=hi)  25.6 us
    dot_general x2, matrix products, local(): back = jnp.einsum('zyx,xw->zyw', ratio, kx, precision=hi)  25.4 us
    dot_general x2, matrix products, local(): returned = jnp.einsum('wc,cyx->wyx', kz_behind, spread, precision=hi)  15.7 us
    ppermute x4, starting transfers between devices, padded(): lax.ppermute(lax.slice_in_dim(block, block.shape[dim] - width, None, axis...  13.6 us
  transfers between devices with their start and end apart: 10, of which 10 were waited for; matrix products, arithmetic and copies ran while one was open for 3% of the time, Pallas kernels for 0%

commit v1 on v0

--- a/solution.py
+++ b/solution.py
@@ -65,7 +65,7 @@
         spread = padded(back, (("blk", 0),), RZ)
         returned = jnp.einsum("wc,cyx->wyx", kz_behind, spread, precision=hi)
         log_terms = jnp.where(inside[:, None, None], jnp.log(returned), jnp.float32(0.0))
-        total = lax.psum(log_terms, "view")
+        total = jnp.sum(lax.all_gather(log_terms, "view"), axis=0)
         estimate = estimate * jnp.exp(total)
     return estimate
 

time: 531 us -> 586 us (1.10)
  the two profiles are of different devices: /device:TPU:8 before, /device:TPU:1 now
where the time goes in v1:
time: 586 us; the launch traced here: 575 us
  waiting for transfers between devices  358 us (61%)
  matrix products  127 us (22%)
  other arithmetic  33.3 us (6%)
  starting transfers between devices  25.4 us (4%)
  local copies, waits for them, and re-layouts  17.3 us (3%)
  between operations  14 us (2%)
    all_gather x2, waiting for transfers between devices, local(): total = jnp.sum(lax.all_gather(log_terms, 'view'), axis=0)  198 us
    ppermute x4, waiting for transfers between devices, padded(): lax.ppermute(lax.slice_in_dim(block, 0, width, axis=dim), axis, backward)  124 us
    ppermute x4, waiting for transfers between devices, padded(): lax.ppermute(lax.slice_in_dim(block, block.shape[dim] - width, None, axis...  35 us
    dot_general x2, matrix products, local(): blurred = jnp.einsum('zyx,wx->zyw', blurred, kx, precision=hi)  27.5 us
    dot_general x2, matrix products, local(): back = jnp.einsum('zyx,xw->zyw', ratio, kx, precision=hi)  25.5 us
    dot_general x2, matrix products, local(): blurred = jnp.einsum('zyx,wy->zwx', blurred, ky, precision=hi)  25.3 us
    dot_general x2, matrix products, local(): back = jnp.einsum('zyx,yw->zwx', back, ky, precision=hi)  25.2 us
    ppermute x4, starting transfers between devices, padded(): lax.ppermute(lax.slice_in_dim(block, block.shape[dim] - width, None, axis...  20.2 us
  transfers between devices with their start and end apart: 10, of which 10 were waited for; matrix products, arithmetic and copies ran while one was open for 3% of the time, Pallas kernels for 0%

profile of v1, /device:TPU:1, one launch (start us, length us, event | category | flops | bytes accessed | tf_op | source)
XLA Modules:
  0.0 574.7 jit_solution(11391682243901679853)
XLA Ops:
  6.5 0.0 all-gather.5.cloned.1.call-start
  6.5 2.8 copy.16
  9.4 5.4 collective-permute-start
  14.7 1.3 collective-permute-start.1
  16.0 0.1 reshape.364
  16.1 0.0 copy-done.4
  16.1 0.6 reduce_sum.49
  16.7 0.6 divide_bitcast_fusion
  17.4 0.0 copy-start
  17.4 4.8 gather_fusion.1
  22.2 0.1 reshape.367
  22.3 0.0 copy-done
  22.3 0.6 slice_reduce_fusion.1
  22.9 1.2 slice_divide_fusion.1
  24.1 0.7 fusion.317
  24.8 0.7 fusion.318
  25.5 32.2 %collective-permute-done = f32[16,128,256]{2,0,1:T(8,128)} collective-permute-done((f32[16,128,256]{2,0,1:T(8,128)S(1)}, f32[16,128,256]{2,0,1:T(8,128)}, u32[]{:S(2)}, u32[]{:S(2)}) %collective-permute-start) | collective-permute-done | bytes 2097184 | tf_op jit(solution)/shard_map/ppermute | solution.py:16
  57.7 5.2 collective-permute-done.1
  62.9 4.9 fusion
  67.8 13.7 %fusion.22 = f32[16,128,256]{2,1,0:T(8,128)S(1)} fusion(f32[16,128,256]{2,0,1:T(8,128)S(1)} %fusion, f32[]{:T(128)} %bitcast.56, f32[]{:T(128)} %bitcast.57, f32[]{:T(128)} %bitcast.58, f32[]{:T(128)} %bitcast.59, f32[]{:T(128)} %bitcast.60, f32[]{:T(128)} %bitcast.62, f32[]{:T(128)} %bitcast.61, f32[]{:T(128)} %bitcast.37, f32[]{:T(128)} %bitcast.39, ...), kind=kOutput, calls=%fused_computation.28 | convolution fusion | flops 1613955072 | bytes 4194372 | tf_op jit(solution)/shard_map/zyx,wx->zyw/dot_general | solution.py:60
  81.5 0.0 copy-start.2
  81.5 12.6 %fusion.78 = f32[128,16,256]{2,0,1:T(8,128)S(1)} fusion(f32[16,128,256]{2,1,0:T(8,128)S(1)} %fusion.22, f32[]{:T(128)} %bitcast.24, f32[]{:T(128)} %bitcast.25, f32[]{:T(128)} %bitcast.26, f32[]{:T(128)} %bitcast.27, f32[]{:T(128)} %bitcast.28, f32[]{:T(128)} %bitcast.30, f32[]{:T(128)} %bitcast.29, f32[]{:T(128)} %bitcast.5, f32[]{:T(128)} %bitcast.7, ...), kind=kOutput, calls=%fused_computation.89 | convolution fusion | flops 806141952 | bytes 4194372 | tf_op jit(solution)/shard_map/zyx,wy->zwx/dot_general | solution.py:61
  94.2 12.7 %fusion.17 = f32[16,128,256]{2,1,0:T(8,128)S(1)} fusion(f32[128,16,256]{2,0,1:T(8,128)S(1)} %fusion.78, f32[1,16,128,256]{3,2,1,0:T(8,128)S(1)} %copy-done.2, f32[]{:T(128)} %bitcast.56, f32[]{:T(128)} %bitcast.57, f32[]{:T(128)} %bitcast.58, f32[]{:T(128)} %bitcast.59, f32[]{:T(128)} %bitcast.60, f32[]{:T(128)} %bitcast.62, f32[]{:T(128)} %bitcast.61, ...), kind=kOutput, calls=%fused_computation.23 | convolution fusion | flops 1614479360 | bytes 6291524 | tf_op jit(solution)/shard_map/zyx,xw->zyw/dot_general | solution.py:63
  106.9 12.5 %convolution_bitcast_fusion.1 = f32[16,128,256]{2,1,0:T(8,128)S(1)} fusion(f32[16,128,256]{2,1,0:T(8,128)S(1)} %fusion.17, f32[]{:T(128)} %bitcast.24, f32[]{:T(128)} %bitcast.25, f32[]{:T(128)} %bitcast.26, f32[]{:T(128)} %bitcast.27, f32[]{:T(128)} %bitcast.28, f32[]{:T(128)} %bitcast.30, f32[]{:T(128)} %bitcast.29, f32[]{:T(128)} %bitcast.5, ...), kind=kOutput, calls=%fused_computation.35 | convolution fusion | flops 806141952 | bytes 4194372 | tf_op jit(solution)/shard_map/zyx,yw->zwx/dot_general | solution.py:64
  119.4 1.3 collective-permute-start.3
  120.7 5.6 collective-permute-start.2
  126.3 0.1 compare_select_fusion.5
  126.4 0.1 reshape.360
  126.5 0.0 copy-start.1
  126.5 4.8 gather_fusion
  131.3 0.1 reshape.363
  131.4 0.0 copy-done.1
  131.4 0.6 fusion.316
  132.0 1.2 compare_and_fusion
  133.2 33.5 %collective-permute-done.3 = f32[16,128,256]{2,1,0:T(8,128)} collective-permute-done((f32[16,128,256]{2,1,0:T(8,128)S(1)}, f32[16,128,256]{2,1,0:T(8,128)}, u32[]{:S(2)}, u32[]{:S(2)}) %collective-permute-start.3) | collective-permute-done | bytes 2097184 | tf_op jit(solution)/shard_map/ppermute | solution.py:19
  166.7 1.1 collective-permute-done.2
  167.8 3.0 pad_maximum_fusion
  170.8 7.8 %log_select_fusion.1 = f32[16,128,256]{2,0,1:T(8,128)} fusion(f32[48,128,256]{2,1,0:T(8,128)S(1)} %pad_maximum_fusion, pred[16]{0:T(512)(128)(4,1)S(1)} %compare_and_fusion, f32[16,48]{1,0:T(8,128)S(1)} %reshape.363, s32[16]{0:T(128)S(1)} %iota_add_fusion.1), kind=kOutput, calls=%fused_computation.33 | convolution fusion | flops 302524160 | bytes 8391760 | tf_op jit(solution)/shard_map/wc,cyx->wyx/dot_general | solution.py:66
  178.6 0.0 all-gather.5.cloned.1.call-update
  178.6 0.0 all-gather.7.cloned.1.call-start
  178.7 100.4 %all-gather.5.cloned.1.call-done = f32[128,128,256]{2,0,1:T(8,128)} async-done(((f32[16,128,256]{2,0,1:T(8,128)}), f32[128,128,256]{2,0,1:T(8,128)}) %all-gather.5.cloned.1.call-update) | async-done | bytes 16777232 | tf_op jit(solution)/shard_map/all_gather | solution.py:68
  279.1 9.8 %reduce_sum.52 = f32[16,128,256]{2,0,1:T(8,128)} reduce(f32[8,16,128,256]{3,1,0,2:T(8,128)} %bitcast.485, f32[]{:T(128)} %constant.28.clone.1), dimensions={0}, to_apply=%region_3.5 | reduce | flops 3670016 | bytes 18874372 | tf_op jit(solution)/shard_map/reduce_sum | solution.py:68
  288.8 3.6 exponential_multiply_fusion.1
  292.4 1.3 collective-permute-start.5
  293.7 4.3 collective-permute-start.4
  298.0 43.3 %collective-permute-done.5 = f32[16,128,256]{2,0,1:T(8,128)S(1)} collective-permute-done((f32[16,128,256]{2,0,1:T(8,128)S(1)}, f32[16,128,256]{2,0,1:T(8,128)S(1)}, u32[]{:S(2)}, u32[]{:S(2)}) %collective-permute-start.5) | collective-permute-done | bytes 2097184 | tf_op jit(solution)/shard_map/ppermute | solution.py:19
  341.3 0.9 collective-permute-done.4
  342.2 3.1 fusion.6
  345.3 13.8 %fusion.20 = f32[16,128,256]{2,1,0:T(8,128)S(1)} fusion(f32[16,128,256]{2,0,1:T(8,128)S(1)} %fusion.6, f32[]{:T(128)} %bitcast.56, f32[]{:T(128)} %bitcast.57, f32[]{:T(128)} %bitcast.58, f32[]{:T(128)} %bitcast.59, f32[]{:T(128)} %bitcast.60, f32[]{:T(128)} %bitcast.62, f32[]{:T(128)} %bitcast.61, f32[]{:T(128)} %bitcast.37, f32[]{:T(128)} %bitcast.39, ...), kind=kOutput, calls=%fused_computation.26 | convolution fusion | flops 1613955072 | bytes 4194372 | tf_op jit(solution)/shard_map/zyx,wx->zyw/dot_general | solution.py:60
  359.1 0.0 copy-start.3
  359.1 12.6 %fusion.76 = f32[128,16,256]{2,0,1:T(8,128)S(1)} fusion(f32[16,128,256]{2,1,0:T(8,128)S(1)} %fusion.20, f32[]{:T(128)} %bitcast.24, f32[]{:T(128)} %bitcast.25, f32[]{:T(128)} %bitcast.26, f32[]{:T(128)} %bitcast.27, f32[]{:T(128)} %bitcast.28, f32[]{:T(128)} %bitcast.30, f32[]{:T(128)} %bitcast.29, f32[]{:T(128)} %bitcast.5, f32[]{:T(128)} %bitcast.7, ...), kind=kOutput, calls=%fused_computation.87 | convolution fusion | flops 806141952 | bytes 4194372 | tf_op jit(solution)/shard_map/zyx,wy->zwx/dot_general | solution.py:61
  371.8 12.8 %fusion.16 = f32[16,128,256]{2,1,0:T(8,128)S(1)} fusion(f32[128,16,256]{2,0,1:T(8,128)S(1)} %fusion.76, f32[1,16,128,256]{3,2,1,0:T(8,128)S(1)} %copy-done.3, f32[]{:T(128)} %bitcast.56, f32[]{:T(128)} %bitcast.57, f32[]{:T(128)} %bitcast.58, f32[]{:T(128)} %bitcast.59, f32[]{:T(128)} %bitcast.60, f32[]{:T(128)} %bitcast.62, f32[]{:T(128)} %bitcast.61, ...), kind=kOutput, calls=%fused_computation.21 | convolution fusion | flops 1614479360 | bytes 6291524 | tf_op jit(solution)/shard_map/zyx,xw->zyw/dot_general | solution.py:63
  384.6 12.7 %convolution_bitcast_fusion = f32[16,128,256]{2,1,0:T(8,128)S(1)} fusion(f32[16,128,256]{2,1,0:T(8,128)S(1)} %fusion.16, f32[]{:T(128)} %bitcast.24, f32[]{:T(128)} %bitcast.25, f32[]{:T(128)} %bitcast.26, f32[]{:T(128)} %bitcast.27, f32[]{:T(128)} %bitcast.28, f32[]{:T(128)} %bitcast.30, f32[]{:T(128)} %bitcast.29, f32[]{:T(128)} %bitcast.5, f32[]{:T(128)} %bitcast.7, ...), kind=kOutput, calls=%fused_computation.34 | convolution fusion | flops 806141952 | bytes 4194372 | tf_op jit(solution)/shard_map/zyx,yw->zwx/dot_general | solution.py:64
  397.3 1.3 collective-permute-start.7
  398.6 4.9 collective-permute-start.6
  403.5 42.5 %collective-permute-done.7 = f32[16,128,256]{2,1,0:T(8,128)S(1)} collective-permute-done((f32[16,128,256]{2,1,0:T(8,128)S(1)}, f32[16,128,256]{2,1,0:T(8,128)S(1)}, u32[]{:S(2)}, u32[]{:S(2)}) %collective-permute-start.7) | collective-permute-done | bytes 2097184 | tf_op jit(solution)/shard_map/ppermute | solution.py:19
  446.0 0.9 collective-permute-done.6
  446.9 0.7 pad_maximum_fusion.1
  447.6 7.8 %log_select_fusion = f32[16,128,256]{2,0,1:T(8,128)} fusion(f32[48,128,256]{2,1,0:T(8,128)S(1)} %pad_maximum_fusion.1, pred[16]{0:T(512)(128)(4,1)S(1)} %compare_and_fusion, f32[16,48]{1,0:T(8,128)S(1)} %reshape.363, s32[16]{0:T(128)S(1)} %iota_add_fusion.1), kind=kOutput, calls=%fused_computation.31 | convolution fusion | flops 302524160 | bytes 8391760 | tf_op jit(solution)/shard_map/wc,cyx->wyx/dot_general | solution.py:66
  455.4 0.0 all-gather.7.cloned.1.call-update
  455.4 97.6 %all-gather.7.cloned.1.call-done = f32[128,128,256]{2,0,1:T(8,128)} async-done(((f32[16,128,256]{2,0,1:T(8,128)}), f32[128,128,256]{2,0,1:T(8,128)}) %all-gather.7.cloned.1.call-update) | async-done | bytes 16777232 | tf_op jit(solution)/shard_map/all_gather | solution.py:68
  553.1 9.8 %reduce_sum.53 = f32[16,128,256]{2,0,1:T(8,128)} reduce(f32[8,16,128,256]{3,1,0,2:T(8,128)} %bitcast.486, f32[]{:T(128)} %constant.28.clone.1), dimensions={0}, to_apply=%region_4.6 | reduce | flops 3670016 | bytes 18874372 | tf_op jit(solution)/shard_map/reduce_sum | solution.py:68
  562.8 2.1 exponential_multiply_fusion
  564.9 2.5 copy.20
  (8 shorter events, 0.0 us)
Async XLA Ops:
  6.5 9.6 %copy-start.4 = (f32[1,33]{1,0:T(1,128)S(1)}, f32[1,33]{1,0:T(1,128)}, u32[]{:S(2)}) copy-start(f32[1,33]{1,0:T(1,128)} %param.9) | copy-start | bytes 400
  6.5 272.5 %all-gather.5.cloned.1.call-start = ((), (), s32[]{:S(2)}) async-start(), calls=%async_computation | async-start | bytes 18874368 | tf_op jit(solution)/shard_map/all_gather | solution.py:68
  9.4 48.3 %collective-permute-start = (f32[16,128,256]{2,0,1:T(8,128)S(1)}, f32[16,128,256]{2,0,1:T(8,128)}, u32[]{:S(2)}, u32[]{:S(2)}) collective-permute-start(f32[16,128,256]{2,0,1:T(8,128)S(1)} %copy.16), channel_id=1, source_target_pairs={{0,8},{8,16},{16,24},{24,32},{32,40},{40,48},{48,56},{56,64},{64,7... | collective-permute-start | bytes 6291464 | tf_op jit(solution)/shard_map/ppermute | solution.py:16
  14.7 48.2 %collective-permute-start.1 = (f32[16,128,256]{2,0,1:T(8,128)S(1)}, f32[16,128,256]{2,0,1:T(8,128)}, u32[]{:S(2)}, u32[]{:S(2)}) collective-permute-start(f32[16,128,256]{2,0,1:T(8,128)S(1)} %copy.16), channel_id=1, source_target_pairs={{8,0},{16,8},{24,16},{32,24},{40,32},{48,40},{56,48},{64,56},{72,6... | collective-permute-start | bytes 6291464 | tf_op jit(solution)/shard_map/ppermute | solution.py:19
  17.4 4.9 copy-start
  81.5 12.6 %copy-start.2 = (f32[1,16,128,256]{3,2,1,0:T(8,128)S(1)}, f32[1,16,128,256]{3,2,1,0:T(8,128)}, u32[]{:S(2)}) copy-start(f32[1,16,128,256]{3,2,1,0:T(8,128)} %param.8) | copy-start | bytes 6291460
  119.4 47.3 %collective-permute-start.3 = (f32[16,128,256]{2,1,0:T(8,128)S(1)}, f32[16,128,256]{2,1,0:T(8,128)}, u32[]{:S(2)}, u32[]{:S(2)}) collective-permute-start(f32[16,128,256]{2,1,0:T(8,128)S(1)} %convolution_bitcast_fusion.1), channel_id=1, source_target_pairs={{8,0},{16,8},{24,16},{32,24},{40,32},{48,40},{56,48},{64,56},{72,6... | collective-permute-start | bytes 6291464 | tf_op jit(solution)/shard_map/ppermute | solution.py:19
  120.7 47.1 %collective-permute-start.2 = (f32[16,128,256]{2,1,0:T(8,128)S(1)}, f32[16,128,256]{2,1,0:T(8,128)}, u32[]{:S(2)}, u32[]{:S(2)}) collective-permute-start(f32[16,128,256]{2,1,0:T(8,128)S(1)} %convolution_bitcast_fusion.1), channel_id=1, source_target_pairs={{0,8},{8,16},{16,24},{24,32},{32,40},{40,48},{48,56},{56,64},{64,7... | collective-permute-start | bytes 6291464 | tf_op jit(solution)/shard_map/ppermute | solution.py:16
  126.5 4.9 copy-start.1
  178.6 374.4 %all-gather.7.cloned.1.call-start = ((), (), s32[]{:S(2)}) async-start(), calls=%async_computation.1 | async-start | bytes 18874368 | tf_op jit(solution)/shard_map/all_gather | solution.py:68
  292.4 48.9 %collective-permute-start.5 = (f32[16,128,256]{2,0,1:T(8,128)S(1)}, f32[16,128,256]{2,0,1:T(8,128)S(1)}, u32[]{:S(2)}, u32[]{:S(2)}) collective-permute-start(f32[16,128,256]{2,0,1:T(8,128)S(1)} %exponential_multiply_fusion.1), channel_id=1, source_target_pairs={{8,0},{16,8},{24,16},{32,24},{40,32},{48,40},{56,48},{64,56},{72,6... | collective-permute-start | bytes 6291464 | tf_op jit(solution)/shard_map/ppermute | solution.py:19
  293.7 48.4 %collective-permute-start.4 = (f32[16,128,256]{2,0,1:T(8,128)S(1)}, f32[16,128,256]{2,0,1:T(8,128)S(1)}, u32[]{:S(2)}, u32[]{:S(2)}) collective-permute-start(f32[16,128,256]{2,0,1:T(8,128)S(1)} %exponential_multiply_fusion.1), channel_id=1, source_target_pairs={{0,8},{8,16},{16,24},{24,32},{32,40},{40,48},{48,56},{56,64},{64,7... | collective-permute-start | bytes 6291464 | tf_op jit(solution)/shard_map/ppermute | solution.py:16
  359.1 12.7 %copy-start.3 = (f32[1,16,128,256]{3,2,1,0:T(8,128)S(1)}, f32[1,16,128,256]{3,2,1,0:T(8,128)}, u32[]{:S(2)}) copy-start(f32[1,16,128,256]{3,2,1,0:T(8,128)} %param.8) | copy-start | bytes 6291460
  397.3 48.7 %collective-permute-start.7 = (f32[16,128,256]{2,1,0:T(8,128)S(1)}, f32[16,128,256]{2,1,0:T(8,128)S(1)}, u32[]{:S(2)}, u32[]{:S(2)}) collective-permute-start(f32[16,128,256]{2,1,0:T(8,128)S(1)} %convolution_bitcast_fusion), channel_id=1, source_target_pairs={{8,0},{16,8},{24,16},{32,24},{40,32},{48,40},{56,48},{64,56},{72,6... | collective-permute-start | bytes 6291464 | tf_op jit(solution)/shard_map/ppermute | solution.py:19
  398.6 48.3 %collective-permute-start.6 = (f32[16,128,256]{2,1,0:T(8,128)S(1)}, f32[16,128,256]{2,1,0:T(8,128)S(1)}, u32[]{:S(2)}, u32[]{:S(2)}) collective-permute-start(f32[16,128,256]{2,1,0:T(8,128)S(1)} %convolution_bitcast_fusion), channel_id=1, source_target_pairs={{0,8},{8,16},{16,24},{24,32},{32,40},{40,48},{48,56},{56,64},{64,7... | collective-permute-start | bytes 6291464 | tf_op jit(solution)/shard_map/ppermute | solution.py:16
Sparse Core Ops, SparseCore 0:
  178.8 100.2 all-gather.4
  455.6 97.4 all-gather.6
